TPU v7x, 32 devices: a whole 2x2x4 slice. The times are simulated.
32 devices in a mesh: seq: 8 (over z, x), tp: 4 (over y, core).
Axes of the slice: x: 2, y: 2, z: 4, core: 2. Of those that a mesh axis runs over, the one named last changes fastest.
Arguments:
- hidden: bfloat16 [2048, 8192], P('seq', 'tp'), may hold values from -6 to 6
- norm_gain: float32 [8192], replicated, may hold values from 0.1 to 1.9
- w_query: bfloat16 [8192, 4096], P('seq', 'tp')
- w_key: bfloat16 [8192, 512], P('seq', 'tp')
- value_weight: bfloat16 [8192, 512], P('seq', 'tp'), may hold values from -0.0625 to 0.0625
- vertical_blocks: int32 [32, 16], replicated, may hold values from 0 to 31, as said below
- slash_offsets: int32 [32, 16], replicated, may hold values from 0 to 31, as said below
- counts: int32 [32, 2], replicated, may hold values from 1 to 16, as said below
Outputs:
- attn_out: bfloat16 [2048, 4096], P('seq', 'tp')
- key_value_cache: bfloat16 [2, 2048, 512], P(None, 'seq', 'tp')
Inputs may be any that keep to these rules, and one draw needn't show every extreme that they name: `vertical_blocks`: the 16 entries of a head are distinct block indices; only the first counts[j, 0] of row j are used. `slash_offsets`: the 16 entries of a head are distinct block offsets, the first of them 0; only the first counts[j, 1] of row j are used. `counts`: column 0 is the number of used vertical blocks, column 1 the number of used slash offsets; some head uses all 16 and all 16.
All inputs are finite; a program needn't handle non-finite values.
Results may differ from a plain program's by a relative error of at most 0.0079.
Values may be sent and summed in bfloat16 or wider, within the bound.
No kernel may reach another device: no remote copies, remote signals or barrier semaphores. Data moves between devices by JAX's collectives and lax.ppermute only.
A program may use at most 128 MiB of HBM per device.

v0:
```python
import jax
import jax.numpy as jnp
from jax import lax
from jax.sharding import PartitionSpec as P

BLOCK = 64
EPSILON = 1e-06
THETA = 1000000.0
NEGATIVE = -1e30


def apply_rotary(value_rows, token_positions, head_width):
    half_width = head_width // 2
    inv_freq = THETA ** (-(jnp.arange(half_width, dtype=jnp.float32) * 2.0) / head_width)
    angles = token_positions.astype(jnp.float32)[:, None] * inv_freq[None, :]
    cosine = jnp.cos(angles)[:, None, :]
    sine_wave = jnp.sin(angles)[:, None, :]
    first_half = value_rows[..., :half_width]
    second = value_rows[..., half_width:]
    return jnp.concatenate(
        [first_half * cosine - second * sine_wave, second * cosine + first_half * sine_wave],
        axis=-1,
    )


def lookup(table_values, head_ids):
    matches = head_ids[:, None] == jnp.arange(table_values.shape[0], dtype=jnp.int32)[None, :]
    return jnp.sum(jnp.where(matches[:, :, None], table_values[None, :, :], 0), axis=1)


def candidates(blocks, head_ids, vertical_blocks, slash_offsets, counts):
    verticals = lookup(vertical_blocks, head_ids)
    slashes = lookup(slash_offsets, head_ids)
    used = lookup(counts, head_ids)
    slash_live = jnp.arange(slashes.shape[1], dtype=jnp.int32)[None, :] < used[:, 1:2]
    slash_rows = blocks[:, None] - slashes
    slash_ok = slash_live & (slash_rows >= 0)
    repeated = jnp.any(
        (blocks[:, None, None] - verticals[:, :, None] == slashes[:, None, :])
        & slash_live[:, None, :],
        axis=2,
    )
    vertical_ok = (
        jnp.arange(verticals.shape[1], dtype=jnp.int32)[None, :] < used[:, 0:1]
    ) & jnp.logical_not(repeated)
    key_blocks = jnp.concatenate([verticals, jnp.maximum(slash_rows, 0)], axis=1)
    block_live = jnp.concatenate([vertical_ok, slash_ok], axis=1)
    return (key_blocks, block_live)


def attend(queries, starts, head_ids, block_table, vertical_blocks, slash_offsets, counts):
    unit_count, row_count, head_width = queries.shape
    key_blocks, block_live = candidates(
        starts // BLOCK, head_ids, vertical_blocks, slash_offsets, counts
    )
    offsets = jnp.arange(BLOCK, dtype=jnp.int32)
    key_pos = (key_blocks[:, :, None] * BLOCK + offsets[None, None, :]).reshape(unit_count, -1)
    key_live = jnp.repeat(block_live, BLOCK, axis=1)
    query_pos = starts[:, None] + jnp.arange(row_count, dtype=jnp.int32)[None, :]
    allowed = key_live[:, None, :] & (key_pos[:, None, :] <= query_pos[:, :, None])
    picked = jnp.take(block_table, key_blocks, axis=0).reshape(unit_count, -1, 2 * head_width)
    picked_keys = picked[:, :, :head_width]
    picked_values = picked[:, :, head_width:]
    scores = jnp.einsum(
        "uqd,ukd->uqk", queries, picked_keys, preferred_element_type=jnp.float32
    ) * head_width ** (-0.5)
    masked = jnp.where(allowed, scores, NEGATIVE)
    row_max = jnp.max(masked, axis=-1, keepdims=True)
    weights = jnp.where(allowed, jnp.exp(masked - row_max), 0.0)
    row_sum = jnp.sum(weights, axis=-1, keepdims=True)
    blended = jnp.einsum(
        "uqk,ukd->uqd",
        weights.astype(jnp.bfloat16),
        picked_values,
        preferred_element_type=jnp.float32,
    )
    return (blended / row_sum).astype(jnp.bfloat16)


def attend_all(
    queries, starts, head_ids, keys_all, values_all, vertical_blocks, slash_offsets, counts
):
    unit_count, unit_rows, head_width = queries.shape
    group_units = max(1, min(unit_count, 512 // unit_rows))
    step_count = unit_count // group_units
    block_table = jnp.concatenate([keys_all, values_all], axis=1).reshape(-1, BLOCK, 2 * head_width)

    def one_group(packed):
        return attend(
            packed[0], packed[1], packed[2], block_table, vertical_blocks, slash_offsets, counts
        )

    result = lax.map(
        one_group,
        (
            queries.reshape(step_count, group_units, unit_rows, head_width),
            starts.reshape(step_count, group_units),
            head_ids.reshape(step_count, group_units),
        ),
    )
    return result.reshape(unit_count, unit_rows, head_width)


def body(hidden, norm_gain, w_query, w_key, value_weight, vertical_blocks, slash_offsets, counts):
    features_all = lax.all_gather(hidden, "tp", axis=1, tiled=True)
    tok_rows = features_all.shape[0]
    widened = features_all.astype(jnp.float32)
    inv_rms = lax.rsqrt(jnp.mean(widened * widened, axis=-1, keepdims=True) + EPSILON)
    normed = (widened * inv_rms * norm_gain[None, :]).astype(jnp.bfloat16)
    head_width = w_key.shape[1]
    heads_here = w_query.shape[1] // head_width
    pieces = (
        lax.all_gather(w_query, "seq", axis=0, tiled=True),
        lax.all_gather(w_key, "seq", axis=0, tiled=True),
        lax.all_gather(value_weight, "seq", axis=0, tiled=True),
    )
    query_proj, key_projected, value_projected = tuple(
        (jnp.dot(normed, panel, preferred_element_type=jnp.float32) for panel in pieces)
    )
    device = lax.axis_index("seq")
    token_positions = device * tok_rows + jnp.arange(tok_rows, dtype=jnp.int32)
    queries = apply_rotary(
        query_proj.reshape(tok_rows, heads_here, head_width), token_positions, head_width
    ).astype(jnp.bfloat16)
    keys_here = (
        apply_rotary(key_projected.reshape(tok_rows, 1, head_width), token_positions, head_width)
        .reshape(tok_rows, head_width)
        .astype(jnp.bfloat16)
    )
    values_here = value_projected.astype(jnp.bfloat16)
    key_value_cache = jnp.stack([keys_here, values_here])
    keys_all, values_all = (
        lax.all_gather(keys_here, "seq", axis=0, tiled=True),
        lax.all_gather(values_here, "seq", axis=0, tiled=True),
    )
    group_base = lax.axis_index("tp") * heads_here
    block_count = tok_rows // BLOCK
    units = jnp.transpose(
        queries.reshape(block_count, BLOCK, heads_here, head_width), (2, 0, 1, 3)
    ).reshape(heads_here * block_count, BLOCK, head_width)
    local_starts = device * tok_rows + jnp.arange(block_count, dtype=jnp.int32) * BLOCK
    starts = jnp.tile(local_starts, heads_here)
    head_ids = group_base + jnp.repeat(jnp.arange(heads_here, dtype=jnp.int32), block_count)
    result = attend_all(
        units, starts, head_ids, keys_all, values_all, vertical_blocks, slash_offsets, counts
    )
    attn_out = jnp.transpose(
        result.reshape(heads_here, block_count, BLOCK, head_width), (1, 2, 0, 3)
    ).reshape(tok_rows, heads_here * head_width)
    return (attn_out, key_value_cache)


def solution(mesh):
    in_specs = (P("seq", "tp"), P(), P("seq", "tp"), P("seq", "tp"), P("seq", "tp"), P(), P(), P())
    out_specs = (P("seq", "tp"), P(None, "seq", "tp"))
    return jax.shard_map(body, mesh=mesh, in_specs=in_specs, out_specs=out_specs, check_vma=False)
```

profile of v0, /device:TPU:0, one launch (start us, length us, event | category | flops | bytes accessed | tf_op | source)
XLA Modules:
  0.0 516.6 jit_solution(12187914340762549450)
XLA Ops:
  10.7 36.0 %all-gather.6.cloned.1.call-done = bf16[256,8192]{1,0:T(8,128)(2,1)} async-done(((bf16[256,2048]{1,0:T(8,128)(2,1)}), bf16[256,8192]{1,0:T(8,128)(2,1)}) %all-gather.6.cloned.1.call-update) | async-done | bytes 4194320 | tf_op jit(solution)/shard_map/all_gather | solution.py:105
  49.9 48.1 %all-gather.10.cloned.1.call-done = bf16[8192,128]{1,0:T(8,128)(2,1)} async-done(((bf16[1024,128]{1,0:T(8,128)(2,1)}), bf16[8192,128]{1,0:T(8,128)(2,1)}) %all-gather.10.cloned.1.call-update) | async-done | bytes 2097168 | tf_op jit(solution)/shard_map/all_gather | solution.py:114
  98.0 4.6 convolution_bitcast_fusion.1
  103.0 32.9 %all-gather = bf16[2048,1,128]{0,2,1:T(8,128)(2,1)S(1)} all-gather(bf16[256,1,128]{0,2,1:T(8,128)(2,1)S(1)} %maximum_convert_fusion), channel_id=2, replica_groups=mesh['seq'=8,'tp'=4] {'seq'}, dimensions={0}, use_global_device_ids=true | all-gather | bytes 589824 | tf_op jit(solution)/shard_map/all_gather | solution.py:133
  135.8 14.3 %all-gather.12.cloned.1.call-done = bf16[8192,128]{1,0:T(8,128)(2,1)} async-done(((bf16[1024,128]{1,0:T(8,128)(2,1)}), bf16[8192,128]{1,0:T(8,128)(2,1)}) %all-gather.12.cloned.1.call-update) | async-done | bytes 2097168 | tf_op jit(solution)/shard_map/all_gather | solution.py:115
  150.1 4.6 convolution_convert_fusion
  154.7 34.0 %all_gather.23 = bf16[2048,128]{0,1:T(8,128)(2,1)S(1)} all-gather(bf16[256,128]{0,1:T(8,128)(2,1)S(1)} %convolution_convert_fusion), channel_id=1, replica_groups=mesh['seq'=8,'tp'=4] {'seq'}, dimensions={0}, use_global_device_ids=true | all-gather | bytes 589824 | tf_op jit(solution)/shard_map/all_gather | solution.py:134
  190.2 191.3 %all-gather.8.cloned.1.call-done = bf16[8192,1024]{1,0:T(8,128)(2,1)} async-done(((bf16[1024,1024]{1,0:T(8,128)(2,1)}), bf16[8192,1024]{1,0:T(8,128)(2,1)}) %all-gather.8.cloned.1.call-update) | async-done | bytes 16777232 | tf_op jit(solution)/shard_map/all_gather | solution.py:113
  381.5 9.4 %convolution_bitcast_fusion = f32[32,8,8,128]{3,1,2,0:T(8,128)S(1)} fusion(bf16[8192,1024]{1,0:T(8,128)(2,1)} %all-gather.8.cloned.1.call-done, bf16[256,8192]{1,0:T(8,128)(2,1)} %all-gather.6.cloned.1.call-done, f32[8192]{0:T(1024)S(1)} %copy-done.3, f32[256]{0:T(256)S(1)} %add_rsqrt_fusion), kind=kOutput, calls=%fused_computation.53 | convolution fusion | flops 4303355904 | bytes 22053888 | tf_op jit(solution)/shard_map/dot_general | solution.py:118
  392.3 116.6 %while.12 = (s32[]{:T(128)}, bf16[4,8,64,128]{3,2,1,0:T(8,128)(2,1)S(1)}, s32[4,8]{1,0:T(4,128)S(1)}, s32[32,2]{0,1:T(2,128)S(1)}, s32[4,8]{1,0:T(4,128)S(1)}, /...) while((s32[]{:T(128)}, ...), condition=%wide.region_8.9_spmd, body=%wide.region_1.8_spmd.sunk | while | flops 551730432 | bytes 47082636 | solution.py:93
  393.0 8.4 %gather_fusion = bf16[256,64,256]{2,1,0:T(8,128)(2,1)} fusion(bf16[32,64,256]{2,1,0:T(8,128)(2,1)S(1)} %get-tuple-element.277, s32[1024]{0:T(1024)S(1)} %pad_clamp_fusion.2), kind=kCustom, calls=%fused_computation.clone.1 | custom fusion | bytes 16778240 | tf_op jit(solution)/shard_map/while/body/eval_jaxpr/jit(_take)/gather | solution.py:61
  401.7 8.0 %bitcast_select_fusion.2 = bf16[8,2048,256]{2,1,0:T(8,128)(2,1)} fusion(pred[8,2048]{1,0:T(8,128)(4,1)S(1)} %broadcast_in_dim.193, bf16[8,2048,256]{2,1,0:T(8,128)(2,1)} %bitcast.68), kind=kLoop, calls=%fused_computation.2.clone.1 | loop fusion | flops 4194304 | bytes 16793600 | tf_op jit(solution)/shard_map/while/body/eval_jaxpr/jit(_take)/select_n | solution.py:61
  411.1 6.6 %fusion.71 = (f32[8,64]{1,0:T(8,128)S(1)}, bf16[8,64,2048]{2,1,0:T(8,128)(2,1)}) fusion(s32[8,64]{1,0:T(8,128)S(1)} %iota_add_fusion.3, s32[8,2048]{1,0:T(8,128)S(1)} %broadcast_add_fusion.2, pred[8,2048]{1,0:T(8,128)(4,1)S(1)} %and.123, bf16[8,2048,256]{2,1,0:T(8,128)(2,1)} %bitcast_select_fusion.2, ...), kind=kOutput, calls=%fused_computation.78.clone.1 | convolution fusion | flops 278923264 | bytes 6597120 | tf_op jit(solution)/shard_map/while/body/eval_jaxpr/sub | solution.py:69
  417.7 3.7 fusion.72
  422.1 8.4 %gather_fusion = bf16[256,64,256]{2,1,0:T(8,128)(2,1)} fusion(bf16[32,64,256]{2,1,0:T(8,128)(2,1)S(1)} %get-tuple-element.277, s32[1024]{0:T(1024)S(1)} %pad_clamp_fusion.2), kind=kCustom, calls=%fused_computation.clone.1 | custom fusion | bytes 16778240 | tf_op jit(solution)/shard_map/while/body/eval_jaxpr/jit(_take)/gather | solution.py:61
  430.8 8.0 %bitcast_select_fusion.2 = bf16[8,2048,256]{2,1,0:T(8,128)(2,1)} fusion(pred[8,2048]{1,0:T(8,128)(4,1)S(1)} %broadcast_in_dim.193, bf16[8,2048,256]{2,1,0:T(8,128)(2,1)} %bitcast.68), kind=kLoop, calls=%fused_computation.2.clone.1 | loop fusion | flops 4194304 | bytes 16793600 | tf_op jit(solution)/shard_map/while/body/eval_jaxpr/jit(_take)/select_n | solution.py:61
  440.2 6.6 %fusion.71 = (f32[8,64]{1,0:T(8,128)S(1)}, bf16[8,64,2048]{2,1,0:T(8,128)(2,1)}) fusion(s32[8,64]{1,0:T(8,128)S(1)} %iota_add_fusion.3, s32[8,2048]{1,0:T(8,128)S(1)} %broadcast_add_fusion.2, pred[8,2048]{1,0:T(8,128)(4,1)S(1)} %and.123, bf16[8,2048,256]{2,1,0:T(8,128)(2,1)} %bitcast_select_fusion.2, ...), kind=kOutput, calls=%fused_computation.78.clone.1 | convolution fusion | flops 278923264 | bytes 6597120 | tf_op jit(solution)/shard_map/while/body/eval_jaxpr/sub | solution.py:69
  446.8 3.7 fusion.72
  451.3 8.4 %gather_fusion = bf16[256,64,256]{2,1,0:T(8,128)(2,1)} fusion(bf16[32,64,256]{2,1,0:T(8,128)(2,1)S(1)} %get-tuple-element.277, s32[1024]{0:T(1024)S(1)} %pad_clamp_fusion.2), kind=kCustom, calls=%fused_computation.clone.1 | custom fusion | bytes 16778240 | tf_op jit(solution)/shard_map/while/body/eval_jaxpr/jit(_take)/gather | solution.py:61
  460.0 8.0 %bitcast_select_fusion.2 = bf16[8,2048,256]{2,1,0:T(8,128)(2,1)} fusion(pred[8,2048]{1,0:T(8,128)(4,1)S(1)} %broadcast_in_dim.193, bf16[8,2048,256]{2,1,0:T(8,128)(2,1)} %bitcast.68), kind=kLoop, calls=%fused_computation.2.clone.1 | loop fusion | flops 4194304 | bytes 16793600 | tf_op jit(solution)/shard_map/while/body/eval_jaxpr/jit(_take)/select_n | solution.py:61
  469.4 6.6 %fusion.71 = (f32[8,64]{1,0:T(8,128)S(1)}, bf16[8,64,2048]{2,1,0:T(8,128)(2,1)}) fusion(s32[8,64]{1,0:T(8,128)S(1)} %iota_add_fusion.3, s32[8,2048]{1,0:T(8,128)S(1)} %broadcast_add_fusion.2, pred[8,2048]{1,0:T(8,128)(4,1)S(1)} %and.123, bf16[8,2048,256]{2,1,0:T(8,128)(2,1)} %bitcast_select_fusion.2, ...), kind=kOutput, calls=%fused_computation.78.clone.1 | convolution fusion | flops 278923264 | bytes 6597120 | tf_op jit(solution)/shard_map/while/body/eval_jaxpr/sub | solution.py:69
  480.4 8.4 %gather_fusion = bf16[256,64,256]{2,1,0:T(8,128)(2,1)} fusion(bf16[32,64,256]{2,1,0:T(8,128)(2,1)S(1)} %get-tuple-element.277, s32[1024]{0:T(1024)S(1)} %pad_clamp_fusion.2), kind=kCustom, calls=%fused_computation.clone.1 | custom fusion | bytes 16778240 | tf_op jit(solution)/shard_map/while/body/eval_jaxpr/jit(_take)/gather | solution.py:61
  489.1 8.0 %bitcast_select_fusion.2 = bf16[8,2048,256]{2,1,0:T(8,128)(2,1)} fusion(pred[8,2048]{1,0:T(8,128)(4,1)S(1)} %broadcast_in_dim.193, bf16[8,2048,256]{2,1,0:T(8,128)(2,1)} %bitcast.68), kind=kLoop, calls=%fused_computation.2.clone.1 | loop fusion | flops 4194304 | bytes 16793600 | tf_op jit(solution)/shard_map/while/body/eval_jaxpr/jit(_take)/select_n | solution.py:61
  498.5 6.6 %fusion.71 = (f32[8,64]{1,0:T(8,128)S(1)}, bf16[8,64,2048]{2,1,0:T(8,128)(2,1)}) fusion(s32[8,64]{1,0:T(8,128)S(1)} %iota_add_fusion.3, s32[8,2048]{1,0:T(8,128)S(1)} %broadcast_add_fusion.2, pred[8,2048]{1,0:T(8,128)(4,1)S(1)} %and.123, bf16[8,2048,256]{2,1,0:T(8,128)(2,1)} %bitcast_select_fusion.2, ...), kind=kOutput, calls=%fused_computation.78.clone.1 | convolution fusion | flops 278923264 | bytes 6597120 | tf_op jit(solution)/shard_map/while/body/eval_jaxpr/sub | solution.py:69
  (148 shorter events, 27.5 us)
Async XLA Ops:
  7.2 90.9 %copy-start.3 = (f32[8192]{0:T(1024)S(1)}, f32[8192]{0:T(1024)}, u32[]{:S(2)}) copy-start(f32[8192]{0:T(1024)} %param.11) | copy-start | bytes 98308
  7.2 39.6 %all-gather.6.cloned.1.call-start = ((), (), s32[]{:S(2)}) async-start(), calls=%async_computation | async-start | bytes 5242880 | tf_op jit(solution)/shard_map/all_gather | solution.py:105
  7.9 90.1 %all-gather.10.cloned.1.call-start = ((), (), s32[]{:S(2)}) async-start(), calls=%async_computation.2 | async-start | bytes 2359296 | tf_op jit(solution)/shard_map/all_gather | solution.py:114
  8.7 141.4 %all-gather.12.cloned.1.call-start = ((), (), s32[]{:S(2)}) async-start(), calls=%async_computation.3 | async-start | bytes 2359296 | tf_op jit(solution)/shard_map/all_gather | solution.py:115
  9.4 372.1 %all-gather.8.cloned.1.call-start = ((), (), s32[]{:S(2)}) async-start(), calls=%async_computation.1 | async-start | bytes 18874368 | tf_op jit(solution)/shard_map/all_gather | solution.py:113
  390.9 1.3 copy-start
  390.9 1.3 copy-start.1
  390.9 1.3 copy-start.2
Sparse Core Ops, SparseCore 0:
  9.5 37.1 all-gather.5
  48.9 49.0 all-gather.9
  100.1 49.9 all-gather.11
  152.1 229.3 all-gather.7
where the time goes:
time: 517 us
  waiting for transfers between devices  292 us (56%)
  blocking collectives  66.9 us (13%)
  matrix products  59.9 us (12%)
  other arithmetic  43 us (8%)
  local copies, waits for them, and re-layouts  40 us (8%)
  between operations  14 us (3%)
    all_gather x1, waiting for transfers between devices, body(): lax.all_gather(w_query, 'seq', axis=0, tiled=True)  191 us
    all_gather x1, waiting for transfers between devices, body(): lax.all_gather(w_key, 'seq', axis=0, tiled=True)  48.1 us
    all_gather x1, waiting for transfers between devices, body(): features_all = lax.all_gather(hidden, 'tp', axis=1, tiled=True)  36 us
    all_gather x1, blocking collectives, body(): lax.all_gather(values_here, 'seq', axis=0, tiled=True)  34 us
    gather x4, local copies, waits for them, and re-layouts, attend(): jnp.take(block_table, key_blocks, axis=0)  33.6 us
    all_gather x1, blocking collectives, body(): lax.all_gather(keys_here, 'seq', axis=0, tiled=True)  32.9 us
    select_n x8, other arithmetic, attend(): jnp.take(block_table, key_blocks, axis=0)  32.4 us
    sub x4, matrix products, attend(): weights = jnp.where(allowed, jnp.exp(masked - row_max), 0.0)  26.5 us
  transfers between devices with their start and end apart: 4, of which 4 were waited for; matrix products, arithmetic and copies ran while one was open for 3% of the time, Pallas kernels for 0%

commit v1 on v0

--- a/solution.py
+++ b/solution.py
@@ -102,7 +102,16 @@
 
 
 def body(hidden, norm_gain, w_query, w_key, value_weight, vertical_blocks, slash_offsets, counts):
-    features_all = lax.all_gather(hidden, "tp", axis=1, tiled=True)
+    peers, mine, span = (lax.axis_size("tp"), lax.axis_index("tp"), hidden.shape[1])
+    right = [(i, (i + 1) % peers) for i in range(peers)]
+    out = jnp.zeros((*hidden.shape[:1], peers * span, *hidden.shape[1 + 1 :]), hidden.dtype)
+    held = hidden
+    for hop in range(peers):
+        holder = (mine - hop) % peers
+        out = lax.dynamic_update_slice_in_dim(out, held, holder * span, axis=1)
+        if hop < peers - 1:
+            held = lax.ppermute(held, "tp", right)
+    features_all = out
     tok_rows = features_all.shape[0]
     widened = features_all.astype(jnp.float32)
     inv_rms = lax.rsqrt(jnp.mean(widened * widened, axis=-1, keepdims=True) + EPSILON)

time: 517 us -> 484 us (0.936)
  waiting for transfers between devices: 292 us -> 256 us
    all_gather x1, waiting for transfers between devices: 48.1 us -> 6 us  [body(): lax.all_gather(w_key, 'seq', axis=0, tiled=True)]
    ppermute x0 -> x3, waiting for transfers between devices: none -> 41.4 us  [body(): held = lax.ppermute(held, 'tp', right)]
    all_gather x1 -> x0, waiting for transfers between devices: 36 us -> none  [body(): features_all = lax.all_gather(hidden, 'tp', axis=1, tiled=True)]
    all_gather x1, waiting for transfers between devices: 14.3 us -> 44.8 us  [body(): lax.all_gather(value_weight, 'seq', axis=0, tiled=True)]
    all_gather x1, waiting for transfers between devices: 191 us -> 161 us  [body(): lax.all_gather(w_query, 'seq', axis=0, tiled=True)]
  transfers between devices with their start and end apart: 4 -> 6, of which waited for: 4 -> 6; matrix products, arithmetic and copies ran while one was open for 3% -> 3% of each run, Pallas kernels for 0% -> 0%
where the time goes in v1:
time: 484 us; the launch traced here: 483 us
  waiting for transfers between devices  256 us (53%)
  blocking collectives  68.5 us (14%)
  matrix products  59.8 us (12%)
  local copies, waits for them, and re-layouts  43 us (9%)
  other arithmetic  40.9 us (8%)
  between operations  14 us (3%)
    all_gather x1, waiting for transfers between devices, body(): lax.all_gather(w_query, 'seq', axis=0, tiled=True)  161 us
    all_gather x1, waiting for transfers between devices, body(): lax.all_gather(value_weight, 'seq', axis=0, tiled=True)  44.8 us
    ppermute x3, waiting for transfers between devices, body(): held = lax.ppermute(held, 'tp', right)  41.4 us
    all_gather x1, blocking collectives, body(): lax.all_gather(keys_here, 'seq', axis=0, tiled=True)  34.6 us
    all_gather x1, blocking collectives, body(): lax.all_gather(values_here, 'seq', axis=0, tiled=True)  33.9 us
    gather x4, local copies, waits for them, and re-layouts, attend(): jnp.take(block_table, key_blocks, axis=0)  33.7 us
    select_n x8, other arithmetic, attend(): jnp.take(block_table, key_blocks, axis=0)  32.4 us
    sub x4, matrix products, attend(): weights = jnp.where(allowed, jnp.exp(masked - row_max), 0.0)  26.5 us
  transfers between devices with their start and end apart: 6, of which 6 were waited for; matrix products, arithmetic and copies ran while one was open for 3% of the time, Pallas kernels for 0%

profile of v1, /device:TPU:0, one launch (start us, length us, event | category | flops | bytes accessed | tf_op | source)
XLA Modules:
  0.0 482.8 jit_solution(6131108125498336317)
XLA Ops:
  9.9 14.6 %collective-permute-done = bf16[256,2048]{1,0:T(8,128)(2,1)S(1)} collective-permute-done((bf16[256,2048]{1,0:T(8,128)(2,1)}, bf16[256,2048]{1,0:T(8,128)(2,1)S(1)}, u32[]{:S(2)}, u32[]{:S(2)}) %collective-permute-start) | collective-permute-done | bytes 1048608 | tf_op jit(solution)/shard_map/ppermute | solution.py:113
  24.8 14.0 %collective-permute-done.1 = bf16[256,2048]{1,0:T(8,128)(2,1)S(1)} collective-permute-done((bf16[256,2048]{1,0:T(8,128)(2,1)S(1)}, bf16[256,2048]{1,0:T(8,128)(2,1)S(1)}, u32[]{:S(2)}, u32[]{:S(2)}) %collective-permute-start.1) | collective-permute-done | bytes 1048608 | tf_op jit(solution)/shard_map/ppermute | solution.py:113
  40.2 12.8 %collective-permute-done.2 = bf16[256,2048]{1,0:T(8,128)(2,1)S(1)} collective-permute-done((bf16[256,2048]{1,0:T(8,128)(2,1)S(1)}, bf16[256,2048]{1,0:T(8,128)(2,1)S(1)}, u32[]{:S(2)}, u32[]{:S(2)}) %collective-permute-start.2) | collective-permute-done | bytes 1048608 | tf_op jit(solution)/shard_map/ppermute | solution.py:113
  56.0 6.0 %all-gather.7.cloned.1.call-done = bf16[8192,128]{1,0:T(8,128)(2,1)} async-done(((bf16[1024,128]{1,0:T(8,128)(2,1)}), bf16[8192,128]{1,0:T(8,128)(2,1)}) %all-gather.7.cloned.1.call-update) | async-done | bytes 2097168 | tf_op jit(solution)/shard_map/all_gather | solution.py:123
  62.0 4.6 convolution_bitcast_fusion.1
  67.0 44.8 %all-gather.9.cloned.1.call-done = bf16[8192,128]{1,0:T(8,128)(2,1)} async-done(((bf16[1024,128]{1,0:T(8,128)(2,1)}), bf16[8192,128]{1,0:T(8,128)(2,1)}) %all-gather.9.cloned.1.call-update) | async-done | bytes 2097168 | tf_op jit(solution)/shard_map/all_gather | solution.py:124
  111.8 4.6 convolution_convert_fusion
  117.2 33.9 %all_gather.19 = bf16[2048,128]{0,1:T(8,128)(2,1)S(1)} all-gather(bf16[256,128]{0,1:T(8,128)(2,1)S(1)} %convolution_convert_fusion), channel_id=1, replica_groups=mesh['seq'=8,'tp'=4] {'seq'}, dimensions={0}, use_global_device_ids=true | all-gather | bytes 589824 | tf_op jit(solution)/shard_map/all_gather | solution.py:143
  151.1 34.6 %all-gather = bf16[2048,1,128]{0,2,1:T(8,128)(2,1)S(1)} all-gather(bf16[256,1,128]{0,2,1:T(8,128)(2,1)S(1)} %maximum_convert_fusion), channel_id=2, replica_groups=mesh['seq'=8,'tp'=4] {'seq'}, dimensions={0}, use_global_device_ids=true | all-gather | bytes 589824 | tf_op jit(solution)/shard_map/all_gather | solution.py:142
  186.3 161.3 %all-gather.5.cloned.1.call-done = bf16[8192,1024]{1,0:T(8,128)(2,1)} async-done(((bf16[1024,1024]{1,0:T(8,128)(2,1)}), bf16[8192,1024]{1,0:T(8,128)(2,1)}) %all-gather.5.cloned.1.call-update) | async-done | bytes 16777232 | tf_op jit(solution)/shard_map/all_gather | solution.py:122
  347.6 9.4 %convolution_bitcast_fusion = f32[32,8,8,128]{3,1,2,0:T(8,128)S(1)} fusion(bf16[8192,1024]{1,0:T(8,128)(2,1)} %all-gather.5.cloned.1.call-done, bf16[256,8192]{1,0:T(8,128)(2,1)} %copy-done, f32[8192]{0:T(1024)S(1)} %copy-done.6, f32[256]{0:T(256)S(1)} %add_rsqrt_fusion), kind=kOutput, calls=%fused_computation.53 | convolution fusion | flops 4303355904 | bytes 22053888 | tf_op jit(solution)/shard_map/dot_general | solution.py:127
  358.4 116.7 %while.12 = (s32[]{:T(128)}, bf16[4,8,64,128]{3,2,1,0:T(8,128)(2,1)S(1)}, s32[4,8]{1,0:T(4,128)S(1)}, s32[32,2]{0,1:T(2,128)S(1)}, s32[4,8]{1,0:T(4,128)S(1)}, /...) while((s32[]{:T(128)}, ...), condition=%wide.region_8.9_spmd, body=%wide.region_1.8_spmd.sunk | while | flops 551730432 | bytes 47082636 | solution.py:93
  359.1 8.4 %gather_fusion = bf16[256,64,256]{2,1,0:T(8,128)(2,1)} fusion(bf16[32,64,256]{2,1,0:T(8,128)(2,1)S(1)} %get-tuple-element.277, s32[1024]{0:T(1024)S(1)} %pad_clamp_fusion.2), kind=kCustom, calls=%fused_computation.clone.1 | custom fusion | bytes 16778240 | tf_op jit(solution)/shard_map/while/body/eval_jaxpr/jit(_take)/gather | solution.py:61
  367.8 8.0 %bitcast_select_fusion.2 = bf16[8,2048,256]{2,1,0:T(8,128)(2,1)} fusion(pred[8,2048]{1,0:T(8,128)(4,1)S(1)} %broadcast_in_dim.197, bf16[8,2048,256]{2,1,0:T(8,128)(2,1)} %bitcast.68), kind=kLoop, calls=%fused_computation.2.clone.1 | loop fusion | flops 4194304 | bytes 16793600 | tf_op jit(solution)/shard_map/while/body/eval_jaxpr/jit(_take)/select_n | solution.py:61
  377.2 6.6 %fusion.71 = (f32[8,64]{1,0:T(8,128)S(1)}, bf16[8,64,2048]{2,1,0:T(8,128)(2,1)}) fusion(s32[8,64]{1,0:T(8,128)S(1)} %iota_add_fusion.3, s32[8,2048]{1,0:T(8,128)S(1)} %broadcast_add_fusion.2, pred[8,2048]{1,0:T(8,128)(4,1)S(1)} %and.144, bf16[8,2048,256]{2,1,0:T(8,128)(2,1)} %bitcast_select_fusion.2, ...), kind=kOutput, calls=%fused_computation.82.clone.1 | convolution fusion | flops 278923264 | bytes 6597120 | tf_op jit(solution)/shard_map/while/body/eval_jaxpr/sub | solution.py:69
  388.2 8.4 %gather_fusion = bf16[256,64,256]{2,1,0:T(8,128)(2,1)} fusion(bf16[32,64,256]{2,1,0:T(8,128)(2,1)S(1)} %get-tuple-element.277, s32[1024]{0:T(1024)S(1)} %pad_clamp_fusion.2), kind=kCustom, calls=%fused_computation.clone.1 | custom fusion | bytes 16778240 | tf_op jit(solution)/shard_map/while/body/eval_jaxpr/jit(_take)/gather | solution.py:61
  397.0 8.0 %bitcast_select_fusion.2 = bf16[8,2048,256]{2,1,0:T(8,128)(2,1)} fusion(pred[8,2048]{1,0:T(8,128)(4,1)S(1)} %broadcast_in_dim.197, bf16[8,2048,256]{2,1,0:T(8,128)(2,1)} %bitcast.68), kind=kLoop, calls=%fused_computation.2.clone.1 | loop fusion | flops 4194304 | bytes 16793600 | tf_op jit(solution)/shard_map/while/body/eval_jaxpr/jit(_take)/select_n | solution.py:61
  406.4 6.6 %fusion.71 = (f32[8,64]{1,0:T(8,128)S(1)}, bf16[8,64,2048]{2,1,0:T(8,128)(2,1)}) fusion(s32[8,64]{1,0:T(8,128)S(1)} %iota_add_fusion.3, s32[8,2048]{1,0:T(8,128)S(1)} %broadcast_add_fusion.2, pred[8,2048]{1,0:T(8,128)(4,1)S(1)} %and.144, bf16[8,2048,256]{2,1,0:T(8,128)(2,1)} %bitcast_select_fusion.2, ...), kind=kOutput, calls=%fused_computation.82.clone.1 | convolution fusion | flops 278923264 | bytes 6597120 | tf_op jit(solution)/shard_map/while/body/eval_jaxpr/sub | solution.py:69
  417.4 8.4 %gather_fusion = bf16[256,64,256]{2,1,0:T(8,128)(2,1)} fusion(bf16[32,64,256]{2,1,0:T(8,128)(2,1)S(1)} %get-tuple-element.277, s32[1024]{0:T(1024)S(1)} %pad_clamp_fusion.2), kind=kCustom, calls=%fused_computation.clone.1 | custom fusion | bytes 16778240 | tf_op jit(solution)/shard_map/while/body/eval_jaxpr/jit(_take)/gather | solution.py:61
  426.2 8.0 %bitcast_select_fusion.2 = bf16[8,2048,256]{2,1,0:T(8,128)(2,1)} fusion(pred[8,2048]{1,0:T(8,128)(4,1)S(1)} %broadcast_in_dim.197, bf16[8,2048,256]{2,1,0:T(8,128)(2,1)} %bitcast.68), kind=kLoop, calls=%fused_computation.2.clone.1 | loop fusion | flops 4194304 | bytes 16793600 | tf_op jit(solution)/shard_map/while/body/eval_jaxpr/jit(_take)/select_n | solution.py:61
  435.6 6.6 %fusion.71 = (f32[8,64]{1,0:T(8,128)S(1)}, bf16[8,64,2048]{2,1,0:T(8,128)(2,1)}) fusion(s32[8,64]{1,0:T(8,128)S(1)} %iota_add_fusion.3, s32[8,2048]{1,0:T(8,128)S(1)} %broadcast_add_fusion.2, pred[8,2048]{1,0:T(8,128)(4,1)S(1)} %and.144, bf16[8,2048,256]{2,1,0:T(8,128)(2,1)} %bitcast_select_fusion.2, ...), kind=kOutput, calls=%fused_computation.82.clone.1 | convolution fusion | flops 278923264 | bytes 6597120 | tf_op jit(solution)/shard_map/while/body/eval_jaxpr/sub | solution.py:69
  446.6 8.4 %gather_fusion = bf16[256,64,256]{2,1,0:T(8,128)(2,1)} fusion(bf16[32,64,256]{2,1,0:T(8,128)(2,1)S(1)} %get-tuple-element.277, s32[1024]{0:T(1024)S(1)} %pad_clamp_fusion.2), kind=kCustom, calls=%fused_computation.clone.1 | custom fusion | bytes 16778240 | tf_op jit(solution)/shard_map/while/body/eval_jaxpr/jit(_take)/gather | solution.py:61
  455.3 8.0 %bitcast_select_fusion.2 = bf16[8,2048,256]{2,1,0:T(8,128)(2,1)} fusion(pred[8,2048]{1,0:T(8,128)(4,1)S(1)} %broadcast_in_dim.197, bf16[8,2048,256]{2,1,0:T(8,128)(2,1)} %bitcast.68), kind=kLoop, calls=%fused_computation.2.clone.1 | loop fusion | flops 4194304 | bytes 16793600 | tf_op jit(solution)/shard_map/while/body/eval_jaxpr/jit(_take)/select_n | solution.py:61
  464.7 6.6 %fusion.71 = (f32[8,64]{1,0:T(8,128)S(1)}, bf16[8,64,2048]{2,1,0:T(8,128)(2,1)}) fusion(s32[8,64]{1,0:T(8,128)S(1)} %iota_add_fusion.3, s32[8,2048]{1,0:T(8,128)S(1)} %broadcast_add_fusion.2, pred[8,2048]{1,0:T(8,128)(4,1)S(1)} %and.144, bf16[8,2048,256]{2,1,0:T(8,128)(2,1)} %bitcast_select_fusion.2, ...), kind=kOutput, calls=%fused_computation.82.clone.1 | convolution fusion | flops 278923264 | bytes 6597120 | tf_op jit(solution)/shard_map/while/body/eval_jaxpr/sub | solution.py:69
  (162 shorter events, 35.6 us)
Async XLA Ops:
  7.2 32.7 %copy-start.1 = (bf16[256,2048]{1,0:T(8,128)(2,1)S(1)}, bf16[256,2048]{1,0:T(8,128)(2,1)}, u32[]{:S(2)}) copy-start(bf16[256,2048]{1,0:T(8,128)(2,1)} %param.10) | copy-start | bytes 3145732
  7.2 54.8 %all-gather.7.cloned.1.call-start = ((), (), s32[]{:S(2)}) async-start(), calls=%async_computation.1 | async-start | bytes 2359296 | tf_op jit(solution)/shard_map/all_gather | solution.py:123
  7.9 103.9 %all-gather.9.cloned.1.call-start = ((), (), s32[]{:S(2)}) async-start(), calls=%async_computation.2 | async-start | bytes 2359296 | tf_op jit(solution)/shard_map/all_gather | solution.py:124
  8.7 338.9 %all-gather.5.cloned.1.call-start = ((), (), s32[]{:S(2)}) async-start(), calls=%async_computation | async-start | bytes 18874368 | tf_op jit(solution)/shard_map/all_gather | solution.py:122
  9.4 15.2 %collective-permute-start = (bf16[256,2048]{1,0:T(8,128)(2,1)}, bf16[256,2048]{1,0:T(8,128)(2,1)S(1)}, u32[]{:S(2)}, u32[]{:S(2)}) collective-permute-start(bf16[256,2048]{1,0:T(8,128)(2,1)} %param.10), channel_id=1, source_target_pairs={{0,1},{1,2},{2,3},{3,0},{4,5},{5,6},{6,7},{7,4},{8,9},{9,10},{10,1... | collective-permute-start | bytes 3145736 | tf_op jit(solution)/shard_map/ppermute | solution.py:113
  24.6 14.2 %collective-permute-start.1 = (bf16[256,2048]{1,0:T(8,128)(2,1)S(1)}, bf16[256,2048]{1,0:T(8,128)(2,1)S(1)}, u32[]{:S(2)}, u32[]{:S(2)}) collective-permute-start(bf16[256,2048]{1,0:T(8,128)(2,1)S(1)} %collective-permute-done), channel_id=1, source_target_pairs={{0,1},{1,2},{2,3},{3,0},{4,5},{5,6},{6,7},{7,4},{8,9},{9,10},{10,1... | collective-permute-start | bytes 3145736 | tf_op jit(solution)/shard_map/ppermute | solution.py:113
  38.8 14.2 %collective-permute-start.2 = (bf16[256,2048]{1,0:T(8,128)(2,1)S(1)}, bf16[256,2048]{1,0:T(8,128)(2,1)S(1)}, u32[]{:S(2)}, u32[]{:S(2)}) collective-permute-start(bf16[256,2048]{1,0:T(8,128)(2,1)S(1)} %collective-permute-done.1), channel_id=1, source_target_pairs={{0,1},{1,2},{2,3},{3,0},{4,5},{5,6},{6,7},{7,4},{8,9},{9,10},{10,1... | collective-permute-start | bytes 3145736 | tf_op jit(solution)/shard_map/ppermute | solution.py:113
  40.1 21.9 %copy-start.6 = (f32[8192]{0:T(1024)S(1)}, f32[8192]{0:T(1024)}, u32[]{:S(2)}) copy-start(f32[8192]{0:T(1024)} %param.11) | copy-start | bytes 98308
  53.1 1.9 copy-start
  357.0 1.3 copy-start.2
  357.0 1.3 copy-start.3
  357.0 1.3 copy-start.4
  357.0 1.3 copy-start.5
Sparse Core Ops, SparseCore 0:
  10.1 51.8 all-gather.6
  64.1 47.6 all-gather.8
  113.9 233.6 all-gather.4
